TPU v7x, 32 devices: a whole 2x2x4 slice. The times are simulated.
32 devices in a mesh: rows: 2 (over y), seq: 16 (over z, x, core).
Axes of the slice: x: 2, y: 2, z: 4, core: 2. Of those that a mesh axis runs over, the one named last changes fastest.
Arguments:
- tokens: bfloat16 [2, 2048, 2304], P('rows', 'seq'), may hold values from -6 to 6
- cotangent: bfloat16 [2, 2048, 2304], P('rows', 'seq'), may hold values from -6 to 6
- doc_ids: int32 [2, 2048], P('rows'), may hold values from 0 to 3, as said below
- bit_levels: int32 [7], replicated, may hold values from 0 to 2, as said below
- w_query: int32 [2304, 2048], P(('rows', 'seq')), may hold values from -128 to 127
- w_key: int32 [2304, 1024], P(('rows', 'seq')), may hold values from -128 to 127
- w_value: int32 [2304, 1024], P(('rows', 'seq')), may hold values from -128 to 127
- w_proj: int32 [2304, 2048], P(('rows', 'seq')), may hold values from -128 to 127
- w_gate: int32 [2304, 9216], P(('rows', 'seq')), may hold values from -128 to 127
- w_up: int32 [2304, 9216], P(('rows', 'seq')), may hold values from -128 to 127
- w_down: int32 [2304, 9216], P(('rows', 'seq')), may hold values from -128 to 127
- gain_first: float32 [2304], replicated, may hold values from -0.5 to 0.5
- gain_second: float32 [2304], replicated, may hold values from -0.5 to 0.5
- gain_third: float32 [2304], replicated, may hold values from -0.5 to 0.5
- gain_fourth: float32 [2304], replicated, may hold values from -0.5 to 0.5
Outputs:
- layer_out: bfloat16 [2, 2048, 2304], P('rows', 'seq')
- grad_tokens: float32 [2, 2048, 2304], P('rows', 'seq')
- grad_query: float32 [2304, 2048], P(('rows', 'seq'))
- grad_key: float32 [2304, 1024], P(('rows', 'seq'))
- grad_value: float32 [2304, 1024], P(('rows', 'seq'))
- grad_proj: float32 [2304, 2048], P(('rows', 'seq'))
- grad_gate: float32 [2304, 9216], P(('rows', 'seq'))
- grad_up: float32 [2304, 9216], P(('rows', 'seq'))
- grad_down: float32 [2304, 9216], P(('rows', 'seq'))
- grad_first: float32 [2304], P(('rows', 'seq'))
- grad_second: float32 [2304], P(('rows', 'seq'))
- grad_third: float32 [2304], P(('rows', 'seq'))
- grad_fourth: float32 [2304], P(('rows', 'seq'))
Inputs may be any that keep to these rules, and one draw needn't show every extreme that they name: `doc_ids`: ids never fall along a row. Rows of even index hold one document (id 0); rows of odd index hold up to four, and their last token has id 3. `bit_levels`: level 0 occurs three times, levels 1 and 2 twice each.
All inputs are finite; a program needn't handle non-finite values.
Results may differ from a plain program's by a relative error of at most 0.019.
The roundings to bfloat16 on the way count: a program that leaves them out, or rounds other values in their place, can miss the bound.
Values may be sent and summed in bfloat16 or wider, within the bound.
A program may use at most 448 MiB of HBM per device.

v0:
```python
import math
import jax
import jax.numpy as jnp
from jax import lax
from jax.sharding import PartitionSpec as P

D = 2304
FF = 9216
HEADS = 8
KV_HEADS = 4
HEAD_DIM = 256
softcap = 50.0
epsilon = 1e-06
qk_boost = 1.65


def dequant(levels_int, level_idx, fan_in, boost):
    stride = jnp.where(level_idx == 0, 1, jnp.where(level_idx == 1, 16, 64)).astype(jnp.int32)
    sliced = levels_int // stride * stride + stride // 2
    return sliced.astype(jnp.float32) * (boost / (74.0 * math.sqrt(fan_in)))


def rmsnorm(values, gain_vec):
    return (
        values
        * lax.rsqrt(jnp.mean(values * values, axis=-1, keepdims=True) + epsilon)
        * (1.0 + gain_vec)
    )


def rotate(values, positions, direction):
    half_dim = HEAD_DIM // 2
    frequency = 10000.0 ** (-(2.0 / HEAD_DIM) * jnp.arange(half_dim, dtype=jnp.float32))
    angles = positions.astype(jnp.float32)[:, None] * frequency[None, :]
    cosine = jnp.cos(angles)[:, None, :]
    sine = jnp.sin(angles)[:, None, :] * direction
    front_half = values[..., :half_dim]
    back_half = values[..., half_dim:]
    return jnp.concatenate(
        [front_half * cosine - back_half * sine, back_half * cosine + front_half * sine], axis=-1
    )


def gelu_product(gate_vals, up_vals):
    return jax.nn.gelu(gate_vals, approximate=True) * up_vals


def per_device(
    tokens,
    cotangent,
    doc_ids,
    bit_levels,
    w_query,
    w_key,
    w_value,
    w_proj,
    w_gate,
    w_up,
    w_down,
    gain_first,
    gain_second,
    gain_third,
    gain_fourth,
):
    rows_here = tokens.shape[0]
    seq_block = tokens.shape[1]
    token_count = rows_here * seq_block
    local_rows = w_query.shape[0]
    group_size = HEADS // KV_HEADS
    query_width = HEADS * HEAD_DIM
    key_width = KV_HEADS * HEAD_DIM
    score_scale = HEAD_DIM ** (-0.5)
    offset = lax.axis_index("seq") * seq_block
    positions = offset + jnp.arange(seq_block, dtype=jnp.int32)
    query_docs = lax.dynamic_slice_in_dim(doc_ids, offset, seq_block, 1)
    query_local = dequant(w_query, bit_levels[0], D, qk_boost).astype(jnp.bfloat16)
    key_local = dequant(w_key, bit_levels[1], D, qk_boost).astype(jnp.bfloat16)
    value_local = dequant(w_value, bit_levels[2], D, 1.0).astype(jnp.bfloat16)
    proj_local = dequant(w_proj, bit_levels[3], query_width, 1.0).astype(jnp.bfloat16)
    gate_local = dequant(w_gate, bit_levels[4], D, 1.0).astype(jnp.bfloat16)
    up_local = dequant(w_up, bit_levels[5], D, 1.0).astype(jnp.bfloat16)
    down_local = dequant(w_down, bit_levels[6], FF, 1.0).astype(jnp.bfloat16)
    query_full, key_full, value_full, proj_full = (
        lax.all_gather(query_local, ("rows", "seq"), axis=0, tiled=True),
        lax.all_gather(key_local, ("rows", "seq"), axis=0, tiled=True),
        lax.all_gather(value_local, ("rows", "seq"), axis=0, tiled=True),
        lax.all_gather(proj_local, ("rows", "seq"), axis=0, tiled=True),
    )
    row_groups = lax.axis_size("rows")
    seq_count = lax.axis_size("seq")
    col_width = FF // seq_count
    stacked = jnp.stack([gate_local, up_local, down_local]).reshape(
        3, local_rows, seq_count, col_width
    )
    spread = jnp.concatenate([stacked] * row_groups, axis=2)
    columns_all = lax.all_to_all(
        spread, ("rows", "seq"), split_axis=2, concat_axis=1, tiled=True
    ).reshape(3, D, col_width)
    gate_cols = columns_all[0]
    up_cols = columns_all[1]
    down_cols = columns_all[2]
    flat_tokens = tokens.astype(jnp.float32).reshape(token_count, D)
    normed_low = rmsnorm(flat_tokens, gain_first).astype(jnp.bfloat16)
    query_pre = jnp.dot(normed_low, query_full, preferred_element_type=jnp.float32)
    key_pre = jnp.dot(normed_low, key_full, preferred_element_type=jnp.float32)
    value_low = (
        jnp.dot(normed_low, value_full, preferred_element_type=jnp.float32)
        .astype(jnp.bfloat16)
        .reshape(rows_here, seq_block, KV_HEADS, HEAD_DIM)
    )
    query_rot = (
        rotate(query_pre.reshape(rows_here, seq_block, HEADS, HEAD_DIM), positions, 1.0)
        .astype(jnp.bfloat16)
        .reshape(rows_here, seq_block, KV_HEADS, group_size, HEAD_DIM)
    )
    key_rot = rotate(
        key_pre.reshape(rows_here, seq_block, KV_HEADS, HEAD_DIM), positions, 1.0
    ).astype(jnp.bfloat16)

    def piece_weights(key_piece):
        key_count = key_piece.shape[1]
        key_pos = jnp.arange(key_count, dtype=jnp.int32)
        raw_scores = (
            jnp.einsum(
                "bqgrd,bkgd->bgrqk", query_rot, key_piece, preferred_element_type=jnp.float32
            )
            * score_scale
        )
        allowed = (key_pos[None, :] <= positions[:, None])[None] & (
            doc_ids[:, None, :] == query_docs[:, :, None]
        )
        bent_score = jnp.tanh(raw_scores / softcap)
        weights = jnp.where(allowed[:, None, None], jnp.exp(softcap * bent_score), 0.0)
        return (weights, bent_score)

    key_piece = lax.all_gather(key_rot, "seq", axis=1, tiled=True)
    value_piece = lax.all_gather(value_low, "seq", axis=1, tiled=True)
    weights, bent_score = piece_weights(key_piece)
    summed = jnp.einsum(
        "bgrqk,bkgd->bqgrd",
        weights.astype(jnp.bfloat16),
        value_piece,
        preferred_element_type=jnp.float32,
    )
    totals, summed = (jnp.sum(weights, axis=-1), summed)
    denominator = jnp.transpose(totals, (0, 3, 1, 2))[..., None]
    mixed_out = summed / denominator
    mixed_low = mixed_out.astype(jnp.bfloat16).reshape(token_count, query_width)
    attn_out = jnp.einsum("th,dh->td", mixed_low, proj_full, preferred_element_type=jnp.float32)
    hidden_one = flat_tokens + rmsnorm(attn_out, gain_second)
    mid_low = rmsnorm(hidden_one, gain_third).astype(jnp.bfloat16)
    mid_row = lax.all_gather(mid_low.reshape(rows_here, seq_block, D), "seq", axis=1, tiled=True)
    gate_pre = jnp.einsum("btd,df->btf", mid_row, gate_cols, preferred_element_type=jnp.float32)
    up_pre = jnp.einsum("btd,df->btf", mid_row, up_cols, preferred_element_type=jnp.float32)
    activated = gelu_product(gate_pre, up_pre).astype(jnp.bfloat16)
    ffn_terms = jnp.einsum("btf,df->btd", activated, down_cols, preferred_element_type=jnp.float32)
    ffn_out = lax.psum_scatter(ffn_terms, "seq", scatter_dimension=1, tiled=True).reshape(
        token_count, D
    )
    result = hidden_one + rmsnorm(ffn_out, gain_fourth)
    layer_out = result.astype(jnp.bfloat16).reshape(rows_here, seq_block, D)
    upstream = cotangent.astype(jnp.float32).reshape(token_count, D)
    grad_ffn, fourth_part = jax.vjp(rmsnorm, ffn_out, gain_fourth)[1](upstream)
    grad_ffn_low = grad_ffn.astype(jnp.bfloat16)
    grad_row = lax.all_gather(
        grad_ffn_low.reshape(rows_here, seq_block, D), "seq", axis=1, tiled=True
    )
    grad_act = jnp.einsum("btd,df->btf", grad_row, down_cols, preferred_element_type=jnp.float32)
    grad_gate_pre, grad_up_pre = jax.vjp(gelu_product, gate_pre, up_pre)[1](grad_act)
    grad_gate_low = grad_gate_pre.astype(jnp.bfloat16)
    grad_up_low = grad_up_pre.astype(jnp.bfloat16)
    mid_terms = jnp.einsum(
        "btf,df->btd", grad_gate_low, gate_cols, preferred_element_type=jnp.float32
    ) + jnp.einsum("btf,df->btd", grad_up_low, up_cols, preferred_element_type=jnp.float32)
    grad_mid = lax.psum_scatter(mid_terms, "seq", scatter_dimension=1, tiled=True).reshape(
        token_count, D
    )
    column_terms = jnp.stack(
        [
            jnp.einsum("btd,btf->df", mid_row, grad_gate_low, preferred_element_type=jnp.float32),
            jnp.einsum("btd,btf->df", mid_row, grad_up_low, preferred_element_type=jnp.float32),
            jnp.einsum("btd,btf->df", grad_row, activated, preferred_element_type=jnp.float32),
        ]
    )
    returned = lax.all_to_all(
        column_terms.reshape(3, D, 1, col_width).astype(jnp.bfloat16),
        ("rows", "seq"),
        split_axis=1,
        concat_axis=2,
        tiled=True,
    ).astype(jnp.float32)
    column_sums = jnp.sum(
        returned.reshape(3, local_rows, row_groups, seq_count, col_width), axis=2
    ).reshape(3, local_rows, FF)
    hidden_part, third_part = jax.vjp(rmsnorm, hidden_one, gain_third)[1](grad_mid)
    grad_hidden = upstream + hidden_part
    grad_attn, second_part = jax.vjp(rmsnorm, attn_out, gain_second)[1](grad_hidden)
    grad_attn_low = grad_attn.astype(jnp.bfloat16)
    query_back, key_back, value_back, proj_back = (
        lax.all_gather(query_local, ("rows", "seq"), axis=0, tiled=True),
        lax.all_gather(key_local, ("rows", "seq"), axis=0, tiled=True),
        lax.all_gather(value_local, ("rows", "seq"), axis=0, tiled=True),
        lax.all_gather(proj_local, ("rows", "seq"), axis=0, tiled=True),
    )
    grad_mixed = jnp.dot(grad_attn_low, proj_back, preferred_element_type=jnp.float32).reshape(
        rows_here, seq_block, KV_HEADS, group_size, HEAD_DIM
    )
    grad_summed = (grad_mixed / denominator).astype(jnp.bfloat16)
    delta_rows = jnp.transpose(
        jnp.sum(grad_mixed * mixed_out, axis=-1) / denominator[..., 0], (0, 2, 3, 1)
    )
    key_piece = lax.all_gather(key_rot, "seq", axis=1, tiled=True)
    value_piece = lax.all_gather(value_low, "seq", axis=1, tiled=True)
    key_count = key_piece.shape[1]
    weights, bent_score = piece_weights(key_piece)
    grad_weights = (
        jnp.einsum(
            "bqgrd,bkgd->bgrqk", grad_summed, value_piece, preferred_element_type=jnp.float32
        )
        - delta_rows[..., None]
    )
    grad_raw = (weights * grad_weights * (1.0 - bent_score * bent_score)).astype(jnp.bfloat16)
    grad_queries = (
        jnp.einsum("bgrqk,bkgd->bqgrd", grad_raw, key_piece, preferred_element_type=jnp.float32)
        * score_scale
    )
    key_term = (
        jnp.einsum("bgrqk,bqgrd->bkgd", grad_raw, query_rot, preferred_element_type=jnp.float32)
        * score_scale
    )
    value_term = jnp.einsum(
        "bgrqk,bqgrd->bkgd",
        weights.astype(jnp.bfloat16),
        grad_summed,
        preferred_element_type=jnp.float32,
    )
    key_sums = key_term
    value_sums = value_term
    grad_query_rot, key_sums, value_sums = (grad_queries, key_sums, value_sums)
    grad_key_rot, grad_value_sum = (
        lax.psum_scatter(key_sums, "seq", scatter_dimension=1, tiled=True),
        lax.psum_scatter(value_sums, "seq", scatter_dimension=1, tiled=True),
    )
    grad_query_pre = (
        rotate(grad_query_rot.reshape(rows_here, seq_block, HEADS, HEAD_DIM), positions, -1.0)
        .astype(jnp.bfloat16)
        .reshape(token_count, query_width)
    )
    grad_key_pre = (
        rotate(grad_key_rot, positions, -1.0).astype(jnp.bfloat16).reshape(token_count, key_width)
    )
    grad_value_low = grad_value_sum.astype(jnp.bfloat16).reshape(token_count, key_width)
    grad_in = (
        jnp.einsum("tf,df->td", grad_query_pre, query_back, preferred_element_type=jnp.float32)
        + jnp.einsum("tf,df->td", grad_key_pre, key_back, preferred_element_type=jnp.float32)
        + jnp.einsum("tf,df->td", grad_value_low, value_back, preferred_element_type=jnp.float32)
    )
    tokens_part, first_part = jax.vjp(rmsnorm, flat_tokens, gain_first)[1](grad_in)
    grad_tokens = (grad_hidden + tokens_part).reshape(rows_here, seq_block, D)

    def outer_sum(left_side, right_side):
        return jnp.einsum("td,tf->df", left_side, right_side, preferred_element_type=jnp.float32)

    gain_terms = jnp.stack([first_part, second_part, third_part, fourth_part], axis=1)
    padding = jnp.zeros((D, 124), jnp.float32)
    weight_terms = jnp.concatenate(
        [
            outer_sum(normed_low, grad_query_pre),
            outer_sum(normed_low, grad_key_pre),
            outer_sum(normed_low, grad_value_low),
            outer_sum(grad_attn_low, mixed_low),
            gain_terms,
            padding,
        ],
        axis=1,
    )
    summed_terms = lax.psum_scatter(weight_terms, ("rows", "seq"), scatter_dimension=0, tiled=True)
    widths = [query_width, key_width, key_width, query_width]
    pieces_out = []
    column = 0
    for span_cols in widths:
        pieces_out.append(summed_terms[:, column : column + span_cols])
        column = column + span_cols
    return (
        layer_out,
        grad_tokens,
        pieces_out[0],
        pieces_out[1],
        pieces_out[2],
        pieces_out[3],
        column_sums[0],
        column_sums[1],
        column_sums[2],
        summed_terms[:, column],
        summed_terms[:, column + 1],
        summed_terms[:, column + 2],
        summed_terms[:, column + 3],
    )


def solution(mesh):
    placed = (
        P("rows", "seq", None),
        P("rows", "seq", None),
        P("rows", None),
        P(),
        P(("rows", "seq"), None),
        P(("rows", "seq"), None),
        P(("rows", "seq"), None),
        P(("rows", "seq"), None),
        P(("rows", "seq"), None),
        P(("rows", "seq"), None),
        P(("rows", "seq"), None),
        P(),
        P(),
        P(),
        P(),
    )
    return jax.shard_map(
        per_device,
        mesh=mesh,
        in_specs=placed,
        out_specs=(
            P("rows", "seq", None),
            P("rows", "seq", None),
            P(("rows", "seq"), None),
            P(("rows", "seq"), None),
            P(("rows", "seq"), None),
            P(("rows", "seq"), None),
            P(("rows", "seq"), None),
            P(("rows", "seq"), None),
            P(("rows", "seq"), None),
            P(("rows", "seq")),
            P(("rows", "seq")),
            P(("rows", "seq")),
            P(("rows", "seq")),
        ),
        check_vma=False,
    )
```

profile of v0, /device:TPU:0, one launch (start us, length us, event | category | flops | bytes accessed | tf_op | source)
XLA Modules:
  0.0 2727.7 jit_solution(16148281413889453011)
XLA Ops:
  32.4 48.7 %all-gather.14.cloned.1.call-done = bf16[2304,1024]{1,0:T(8,128)(2,1)} async-done(((bf16[72,1024]{1,0:T(8,128)(2,1)}), bf16[2304,1024]{1,0:T(8,128)(2,1)}) %all-gather.14.cloned.1.call-update) | async-done | bytes 4718608 | tf_op jit(solution)/shard_map/all_gather | solution.py:85
  92.8 54.2 %all-gather.10.cloned.1.call-done = bf16[2304,1024]{1,0:T(8,128)(2,1)} async-done(((bf16[72,1024]{1,0:T(8,128)(2,1)}), bf16[2304,1024]{1,0:T(8,128)(2,1)}) %all-gather.10.cloned.1.call-update) | async-done | bytes 4718608 | tf_op jit(solution)/shard_map/all_gather | solution.py:86
  166.9 27.3 %fusion.38 = bf16[72,9216]{1,0:T(8,128)(2,1)} fusion(s32[72,9216]{1,0:T(8,128)S(1)} %copy-done.13, s32[]{:T(128)S(6)} %select_n.149, s32[]{:T(128)} %bitcast.33, s32[]{:T(128)S(6)} %sign.73), kind=kLoop, calls=%fused_computation.56 | loop fusion | flops 8626176 | bytes 3981324 | tf_op jit(solution)/shard_map/convert_element_type | solution.py:80
  194.2 27.7 %fusion.48 = bf16[72,9216]{1,0:T(8,128)(2,1)} fusion(s32[72,9216]{1,0:T(8,128)S(1)} %copy-done.14, s32[]{:T(128)S(6)} %select_n.159, s32[]{:T(128)} %bitcast.35, s32[]{:T(128)S(6)} %sign.77), kind=kLoop, calls=%fused_computation.66 | loop fusion | flops 8626176 | bytes 3981324 | tf_op jit(solution)/shard_map/convert_element_type | solution.py:82
  231.2 12.8 copy.124
  251.2 32.2 %all-gather.16.cloned.1.call-done = bf16[1,2048,4,256]{3,1,2,0:T(8,128)(2,1)} async-done(((bf16[1,128,4,256]{3,1,2,0:T(8,128)(2,1)}), bf16[1,2048,4,256]{3,1,2,0:T(8,128)(2,1)}) %all-gather.16.cloned.1.call-update) | async-done | bytes 4194320 | tf_op jit(solution)/shard_map/all_gather | solution.py:136
  290.4 47.3 %all-gather.12.cloned.1.call-done = bf16[1,2048,4,256]{1,3,2,0:T(8,128)(2,1)} async-done(((bf16[1,128,4,256]{1,3,2,0:T(8,128)(2,1)}), bf16[1,2048,4,256]{1,3,2,0:T(8,128)(2,1)}) %all-gather.12.cloned.1.call-update) | async-done | bytes 4194320 | tf_op jit(solution)/shard_map/all_gather | solution.py:137
  346.1 75.1 %all-gather.20.cloned.1.call-done = bf16[2304,2048]{1,0:T(8,128)(2,1)} async-done(((bf16[72,2048]{1,0:T(8,128)(2,1)}), bf16[2304,2048]{1,0:T(8,128)(2,1)}) %all-gather.20.cloned.1.call-update) | async-done | bytes 9437200 | tf_op jit(solution)/shard_map/all_gather | solution.py:87
  429.7 29.0 %fusion.43 = bf16[72,9216]{1,0:T(8,128)(2,1)} fusion(s32[72,9216]{1,0:T(8,128)} %param.24, s32[]{:T(128)S(6)} %select_n.154, s32[]{:T(128)} %bitcast.34, s32[]{:T(128)S(6)} %sign.75), kind=kLoop, calls=%fused_computation.61 | loop fusion | flops 8626176 | bytes 3981324 | tf_op jit(solution)/shard_map/convert_element_type | solution.py:81
  469.5 9.6 maximum_maximum_fusion
  479.1 10.2 copy.126
  489.3 209.2 %all_to_all.24 = bf16[3,72,32,576]{3,1,0,2:T(8,128)(2,1)S(1)} all-to-all(bf16[3,72,32,576]{3,1,0,2:T(8,128)(2,1)} %copy.126), channel_id=1, replica_groups=mesh['rows'=2,'seq'=16] {'rows','seq'}, dimensions={2} | all-to-all | bytes 15925248 | tf_op jit(solution)/shard_map/all_to_all | solution.py:96
  711.6 12.6 multiply_convert_fusion.1
  725.6 10.9 convolution_bitcast_fusion
  737.2 191.9 %reduce-scatter.6.cloned.1.call-done = f32[1,128,2304]{2,1,0:T(8,128)} async-done(((f32[1,2048,2304]{2,1,0:T(8,128)}), f32[1,128,2304]{2,1,0:T(8,128)}) %reduce-scatter.6.cloned.1.call-update) | async-done | bytes 1179664 | tf_op jit(solution)/shard_map/reduce_scatter | solution.py:157
  934.7 80.7 %all-gather.22.cloned.1.call-done = bf16[1,2048,2304]{2,1,0:T(8,128)(2,1)} async-done(((bf16[1,128,2304]{2,1,0:T(8,128)(2,1)}), bf16[1,2048,2304]{2,1,0:T(8,128)(2,1)}) %all-gather.22.cloned.1.call-update) | async-done | bytes 9437200 | tf_op jit(solution)/shard_map/all_gather | solution.py:165
  1015.3 16.0 multiply_convert_fusion
  1031.3 10.8 fusion.155
  1042.2 19.0 add_bitcast_fusion
  1061.3 193.2 %reduce-scatter.8.cloned.1.call-done = f32[1,128,2304]{2,1,0:T(8,128)} async-done(((f32[1,2048,2304]{2,1,0:T(8,128)}), f32[1,128,2304]{2,1,0:T(8,128)}) %reduce-scatter.8.cloned.1.call-update) | async-done | bytes 1179664 | tf_op jit(solution)/shard_map/reduce_scatter | solution.py:175
  1278.5 10.0 convolution_bitcast_fusion.1
  1321.3 61.2 %reduce-scatter.10.cloned.1.call-done = f32[1,128,4,256]{3,1,2,0:T(8,128)} async-done(((f32[1,2048,4,256]{3,1,2,0:T(8,128)}), f32[1,128,4,256]{3,1,2,0:T(8,128)}) %reduce-scatter.10.cloned.1.call-update) | async-done | bytes 524304 | tf_op jit(solution)/shard_map/reduce_scatter | solution.py:241
  1383.8 107.2 %reduce-scatter.12.cloned.1.call-done = f32[1,128,4,256]{1,3,2,0:T(8,128)} async-done(((f32[1,2048,4,256]{1,3,2,0:T(8,128)}), f32[1,128,4,256]{1,3,2,0:T(8,128)}) %reduce-scatter.12.cloned.1.call-update) | async-done | bytes 524304 | tf_op jit(solution)/shard_map/reduce_scatter | solution.py:242
  1508.1 132.7 %concatenate.69 = f32[2304,6272]{0,1:T(8,128)} concatenate(f32[2304,2048]{0,1:T(8,128)} %fusion.111, f32[2304,1024]{0,1:T(8,128)} %fusion.113, f32[2304,1024]{0,1:T(8,128)} %fusion.109, f32[2304,2048]{0,1:T(8,128)} %fusion.158, f32[2304,1]{0,1:T(1,128)S(1)} %stack.40, f32[2304,1]{0,1:T(1,128)S(1)} %copy-done.29, f32[2304,1]{0,1:T(1,128)S(1)} %copy-done.28, ...), dimensions={1} | concatenate | bytes 115605504 | tf_op jit(solution)/shard_map/concatenate | solution.py:266
  1642.5 9.8 fusion.19
  1652.3 10.1 fusion.23
  1672.2 19.6 copy.140
  1696.3 380.9 %all-to-all-done.1 = bf16[3,2304,1,576]{3,0,2,1:T(4,128)(2,1)} async-done(((bf16[3,2304,1,576]{3,0,2,1:T(4,128)(2,1)}), bf16[3,2304,1,576]{3,0,2,1:T(4,128)(2,1)}, u32[]{:S(2)}, u32[]{:S(2)}) %all-to-all-start.1) | async-done | bytes 7962656 | tf_op jit(solution)/shard_map/all_to_all | solution.py:185
  2077.1 9.6 copy.141
  2086.7 11.0 convert.36
  2097.7 12.1 reduce_sum.170
  2137.5 573.2 %all-reduce.3.cloned.1.call-done = f32[2304,6272]{0,1:T(8,128)} async-done(((f32[2304,6272]{0,1:T(8,128)}), f32[2304,6272]{0,1:T(8,128)}) %all-reduce.3.cloned.1.call-update) | async-done | bytes 57802768
  (231 shorter events, 248.0 us)
Async XLA Ops:
  7.2 24.2 copy-start.32
  7.2 73.9 %all-gather.14.cloned.1.call-start = ((), (), s32[]{:S(2)}) async-start(), calls=%async_computation.8 | async-start | bytes 4866048 | tf_op jit(solution)/shard_map/all_gather | solution.py:85
  14.6 132.3 %all-gather.10.cloned.1.call-start = ((), (), s32[]{:S(2)}) async-start(), calls=%async_computation.6 | async-start | bytes 4866048 | tf_op jit(solution)/shard_map/all_gather | solution.py:86
  20.6 210.7 %all-gather.18.cloned.1.call-start = ((), (), s32[]{:S(2)}) async-start(), calls=%async_computation.10 | async-start | bytes 9732096 | tf_op jit(solution)/shard_map/all_gather | solution.py:84
  30.1 253.3 %all-gather.16.cloned.1.call-start = ((), (), s32[]{:S(2)}) async-start(), calls=%async_computation.9 | async-start | bytes 4456448 | tf_op jit(solution)/shard_map/all_gather | solution.py:136
  31.4 56.4 %copy-start.38 = (f32[128]{0:T(128)}, f32[128]{0:T(128)S(1)}, u32[]{:S(2)}) copy-start(f32[128]{0:T(128)S(1)} %fusion.77) | copy-start | bytes 1540
  31.4 212.6 %copy-start.30 = (f32[128]{0:T(128)}, f32[128]{0:T(128)S(1)}, u32[]{:S(2)}) copy-start(f32[128]{0:T(128)S(1)} %fusion.132) | copy-start | bytes 1540
  31.4 212.6 %copy-start.22 = (f32[2304]{0:T(1024)}, f32[2304]{0:T(1024)S(1)}, u32[]{:S(2)}) copy-start(f32[2304]{0:T(1024)S(1)} %broadcast_add_fusion.3) | copy-start | bytes 27652
  32.4 218.6 %copy-start.17 = (f32[128,128]{1,0:T(8,128)}, f32[128,128]{1,0:T(8,128)S(1)}, u32[]{:S(2)}) copy-start(f32[128,128]{1,0:T(8,128)S(1)} %get-tuple-element.116) | copy-start | bytes 196612
  92.7 73.1 %copy-start.36 = (s32[1,2048]{1,0:T(1,128)S(1)}, s32[1,2048]{1,0:T(1,128)}, u32[]{:S(2)}) copy-start(s32[1,2048]{1,0:T(1,128)} %param.17) | copy-start | bytes 24580
  92.7 73.1 %copy-start.33 = (f32[2304]{0:T(1024)S(1)}, f32[2304]{0:T(1024)}, u32[]{:S(2)}) copy-start(f32[2304]{0:T(1024)} %param.27) | copy-start | bytes 27652
  92.7 73.2 %copy-start.34 = (f32[2304]{0:T(1024)S(1)}, f32[2304]{0:T(1024)}, u32[]{:S(2)}) copy-start(f32[2304]{0:T(1024)} %param.28) | copy-start | bytes 27652
  92.7 74.2 %copy-start.13 = (s32[72,9216]{1,0:T(8,128)S(1)}, s32[72,9216]{1,0:T(8,128)}, u32[]{:S(2)}) copy-start(s32[72,9216]{1,0:T(8,128)} %param.23) | copy-start | bytes 7962628
  92.7 245.0 %all-gather.12.cloned.1.call-start = ((), (), s32[]{:S(2)}) async-start(), calls=%async_computation.7 | async-start | bytes 4456448 | tf_op jit(solution)/shard_map/all_gather | solution.py:137
  152.6 268.6 %all-gather.20.cloned.1.call-start = ((), (), s32[]{:S(2)}) async-start(), calls=%async_computation.11 | async-start | bytes 9732096 | tf_op jit(solution)/shard_map/all_gather | solution.py:87
  161.8 540.3 %all-gather.24.cloned.1.call-start = ((), (), s32[]{:S(2)}) async-start(), calls=%async_computation.17 | async-start | bytes 10027008 | tf_op jit(solution)/shard_map/all_gather | solution.py:152
  165.8 28.5 %copy-start.14 = (s32[72,9216]{1,0:T(8,128)S(1)}, s32[72,9216]{1,0:T(8,128)}, u32[]{:S(2)}) copy-start(s32[72,9216]{1,0:T(8,128)} %param.25) | copy-start | bytes 7962628
  244.0 39.3 %copy-start.25 = (pred[128,2048]{0,1:T(8,128)(4,1)S(1)}, pred[128,2048]{0,1:T(8,128)(4,1)}, u32[]{:S(2)}) copy-start(pred[128,2048]{0,1:T(8,128)(4,1)} %fusion.91) | copy-start | bytes 786436
  251.1 39.3 %copy-start.20 = (bf16[1,128,8,128]{3,1,2,0:T(8,128)(2,1)}, bf16[1,128,8,128]{3,1,2,0:T(8,128)(2,1)S(1)}, u32[]{:S(2)}) copy-start(bf16[1,128,8,128]{3,1,2,0:T(8,128)(2,1)S(1)} %get-tuple-element.109) | copy-start | bytes 786436
  346.1 82.1 %copy-start.15 = (bf16[1,128,4,2,256]{1,4,3,2,0:T(8,128)(2,1)}, bf16[1,128,4,2,256]{1,4,3,2,0:T(8,128)(2,1)S(1)}, u32[]{:S(2)}) copy-start(bf16[1,128,4,2,256]{1,4,3,2,0:T(8,128)(2,1)S(1)} %get-tuple-element.126) | copy-start | bytes 1572868
  429.6 499.5 %reduce-scatter.6.cloned.1.call-start = ((), (), s32[]{:S(2)}) async-start(), calls=%async_computation.12 | async-start | bytes 20054016 | tf_op jit(solution)/shard_map/reduce_scatter | solution.py:157
  711.5 14.1 copy-start.12
  736.5 194.1 %copy-start.6 = (bf16[1,128,2304]{2,1,0:T(8,128)(2,1)S(1)}, bf16[1,128,2304]{2,1,0:T(8,128)(2,1)}, u32[]{:S(2)}) copy-start(bf16[1,128,2304]{2,1,0:T(8,128)(2,1)} %param.16) | copy-start | bytes 1769476
  736.5 278.8 %all-gather.22.cloned.1.call-start = ((), (), s32[]{:S(2)}) async-start(), calls=%async_computation.13 | async-start | bytes 10027008 | tf_op jit(solution)/shard_map/all_gather | solution.py:165
  934.6 319.8 %reduce-scatter.8.cloned.1.call-start = ((), (), s32[]{:S(2)}) async-start(), calls=%async_computation.14 | async-start | bytes 20054016 | tf_op jit(solution)/shard_map/reduce_scatter | solution.py:175
  1015.3 16.0 copy-start.11
  1061.2 321.2 %reduce-scatter.10.cloned.1.call-start = ((), (), s32[]{:S(2)}) async-start(), calls=%async_computation.15 | async-start | bytes 8912896 | tf_op jit(solution)/shard_map/reduce_scatter | solution.py:241
  1278.5 212.5 %reduce-scatter.12.cloned.1.call-start = ((), (), s32[]{:S(2)}) async-start(), calls=%async_computation.16 | async-start | bytes 8912896 | tf_op jit(solution)/shard_map/reduce_scatter | solution.py:242
  1288.5 1422.2 %all-reduce.3.cloned.1.call-start = ((), (), s32[]{:S(2)}) async-start(), calls=%async_computation.18 | async-start | bytes 115605504
  1642.5 19.9 slice-start.4
  1642.5 19.9 slice-start.5
  1691.8 385.4 %all-to-all-start.1 = ((bf16[3,2304,1,576]{3,0,2,1:T(4,128)(2,1)}), bf16[3,2304,1,576]{3,0,2,1:T(4,128)(2,1)}, u32[]{:S(2)}, u32[]{:S(2)}) async-start(bf16[3,2304,1,576]{3,0,2,1:T(4,128)(2,1)} %copy.140), calls=%async_computation.5 | async-start | bytes 23592960 | tf_op jit(solution)/shard_map/all_to_all | solution.py:185
  (36 other events, 230.3 us)
Sparse Core Ops, SparseCore 0:
  14.8 66.2 all-gather.13
  84.5 62.3 all-gather.9
  150.4 80.7 all-gather.17
  233.9 49.4 all-gather.15
  285.9 51.6 all-gather.11
  341.0 80.1 all-gather.19
  429.7 95.4 all-gather.23
  736.6 192.4 reduce-scatter.5
  934.7 80.5 all-gather.21
  1061.4 193.0 reduce-scatter.7
  1278.6 103.8 reduce-scatter.9
  1386.4 104.5 reduce-scatter.11
  1641.0 1069.6 all-reduce.2
where the time goes:
time: 2740 us; the launch traced here: 2730 us
  waiting for transfers between devices  1860 us (68%)
  local copies, waits for them, and re-layouts  255 us (9%)
  matrix products  216 us (8%)
  blocking collectives  209 us (8%)
  other arithmetic  163 us (6%)
    unnamed x14, waiting for transfers between devices  573 us
    all_to_all x1, waiting for transfers between devices, per_device(): lax.all_to_all(column_terms.reshape(3, D, 1, col_width).astype(jnp.bfloat...  381 us
    all_to_all x1, blocking collectives, per_device(): lax.all_to_all(spread, ('rows', 'seq'), split_axis=2, concat_axis=1, tile...  209 us
    reduce_scatter x1, waiting for transfers between devices, per_device(): lax.psum_scatter(mid_terms, 'seq', scatter_dimension=1, tiled=True)  193 us
    reduce_scatter x1, waiting for transfers between devices, per_device(): lax.psum_scatter(ffn_terms, 'seq', scatter_dimension=1, tiled=True)  192 us
    concatenate x1, local copies, waits for them, and re-layouts, per_device(): jnp.concatenate([outer_sum(normed_low, grad_query_pre), outer_sum(normed_...  133 us
    reduce_scatter x1, waiting for transfers between devices, per_device(): lax.psum_scatter(value_sums, 'seq', scatter_dimension=1, tiled=True)  107 us
    all_gather x1, waiting for transfers between devices, per_device(): lax.all_gather(grad_ffn_low.reshape(rows_here, seq_block, D), 'seq', axis...  80.7 us
  transfers between devices with their start and end apart: 14, of which 13 were waited for; matrix products, arithmetic and copies ran while one was open for 13% of the time, Pallas kernels for 0%

commit v1 on v0

--- a/solution.py
+++ b/solution.py
@@ -133,8 +133,11 @@
         weights = jnp.where(allowed[:, None, None], jnp.exp(softcap * bent_score), 0.0)
         return (weights, bent_score)
 
-    key_piece = lax.all_gather(key_rot, "seq", axis=1, tiled=True)
-    value_piece = lax.all_gather(value_low, "seq", axis=1, tiled=True)
+    key_piece, value_piece = jnp.split(
+        lax.all_gather(jnp.concatenate([key_rot, value_low], axis=0), "seq", axis=1, tiled=True),
+        [key_rot.shape[0]],
+        axis=0,
+    )
     weights, bent_score = piece_weights(key_piece)
     summed = jnp.einsum(
         "bgrqk,bkgd->bqgrd",

time: 2740 us -> 2760 us (level)
    all_gather x0 -> x1, waiting for transfers between devices: none -> 56.3 us  [per_device(): lax.all_gather(jnp.concatenate([key_rot, value_low], axis=0), 'seq', axis...]
    all_gather x1, waiting for transfers between devices: 32.2 us -> 4.29 us  [per_device(): key_piece = lax.all_gather(key_rot, 'seq', axis=1, tiled=True)]
    unnamed x14 -> x15, waiting for transfers between devices: 573 us -> 574 us
  transfers between devices with their start and end apart: 14 -> 15, of which waited for: 13 -> 14; matrix products, arithmetic and copies ran while one was open for 13% -> 15% of each run, Pallas kernels for 0% -> 0%
where the time goes in v1:
time: 2760 us; the launch traced here: 2750 us
  waiting for transfers between devices  1880 us (68%)
  local copies, waits for them, and re-layouts  254 us (9%)
  matrix products  215 us (8%)
  blocking collectives  209 us (8%)
  other arithmetic  164 us (6%)
    unnamed x15, waiting for transfers between devices  574 us
    all_to_all x1, waiting for transfers between devices, per_device(): lax.all_to_all(column_terms.reshape(3, D, 1, col_width).astype(jnp.bfloat...  381 us
    all_to_all x1, blocking collectives, per_device(): lax.all_to_all(spread, ('rows', 'seq'), split_axis=2, concat_axis=1, tile...  209 us
    reduce_scatter x1, waiting for transfers between devices, per_device(): lax.psum_scatter(ffn_terms, 'seq', scatter_dimension=1, tiled=True)  192 us
    reduce_scatter x1, waiting for transfers between devices, per_device(): lax.psum_scatter(mid_terms, 'seq', scatter_dimension=1, tiled=True)  191 us
    concatenate x1, local copies, waits for them, and re-layouts, per_device(): jnp.concatenate([outer_sum(normed_low, grad_query_pre), outer_sum(normed_...  133 us
    reduce_scatter x1, waiting for transfers between devices, per_device(): lax.psum_scatter(value_sums, 'seq', scatter_dimension=1, tiled=True)  107 us
    all_gather x1, waiting for transfers between devices, per_device(): lax.all_gather(grad_ffn_low.reshape(rows_here, seq_block, D), 'seq', axis...  78.9 us
  transfers between devices with their start and end apart: 15, of which 14 were waited for; matrix products, arithmetic and copies ran while one was open for 15% of the time, Pallas kernels for 0%

profile of v1, /device:TPU:0, one launch (start us, length us, event | category | flops | bytes accessed | tf_op | source)
XLA Modules:
  0.0 2748.9 jit_solution(3117528931341905655)
XLA Ops:
  32.5 48.6 %all-gather.13.cloned.1.call-done = bf16[2304,1024]{1,0:T(8,128)(2,1)} async-done(((bf16[72,1024]{1,0:T(8,128)(2,1)}), bf16[2304,1024]{1,0:T(8,128)(2,1)}) %all-gather.13.cloned.1.call-update) | async-done | bytes 4718608 | tf_op jit(solution)/shard_map/all_gather | solution.py:86
  84.6 62.4 %all-gather.11.cloned.1.call-done = bf16[2304,1024]{1,0:T(8,128)(2,1)} async-done(((bf16[72,1024]{1,0:T(8,128)(2,1)}), bf16[2304,1024]{1,0:T(8,128)(2,1)}) %all-gather.11.cloned.1.call-update) | async-done | bytes 4718608 | tf_op jit(solution)/shard_map/all_gather | solution.py:85
  173.7 27.3 fusion.50
  201.0 27.6 %fusion.60 = bf16[72,9216]{1,0:T(8,128)(2,1)} fusion(s32[72,9216]{1,0:T(8,128)S(1)} %copy-done.14, s32[]{:T(128)S(6)} %select_n.161, s32[]{:T(128)} %bitcast.34, s32[]{:T(128)S(6)} %sign.77), kind=kLoop, calls=%fused_computation.79 | loop fusion | flops 8626176 | bytes 3981324 | tf_op jit(solution)/shard_map/convert_element_type | solution.py:82
  231.5 12.7 copy.130
  251.4 56.3 %all-gather.15.cloned.1.call-done = bf16[2,2048,4,256]{3,1,2,0:T(8,128)(2,1)} async-done(((bf16[2,128,4,256]{3,1,2,0:T(8,128)(2,1)}), bf16[2,2048,4,256]{3,1,2,0:T(8,128)(2,1)}) %all-gather.15.cloned.1.call-update) | async-done | bytes 8388624 | tf_op jit(solution)/shard_map/all_gather | solution.py:137
  316.3 75.0 %all-gather.19.cloned.1.call-done = bf16[2304,2048]{1,0:T(8,128)(2,1)} async-done(((bf16[72,2048]{1,0:T(8,128)(2,1)}), bf16[2304,2048]{1,0:T(8,128)(2,1)}) %all-gather.19.cloned.1.call-update) | async-done | bytes 9437200 | tf_op jit(solution)/shard_map/all_gather | solution.py:87
  399.7 29.0 %fusion.55 = bf16[72,9216]{1,0:T(8,128)(2,1)} fusion(s32[72,9216]{1,0:T(8,128)} %param.24, s32[]{:T(128)S(6)} %select_n.156, s32[]{:T(128)} %bitcast.33, s32[]{:T(128)S(6)} %sign.75), kind=kLoop, calls=%fused_computation.74 | loop fusion | flops 8626176 | bytes 3981324 | tf_op jit(solution)/shard_map/convert_element_type | solution.py:81
  439.5 9.6 maximum_maximum_fusion
  449.1 10.2 copy.133
  459.3 209.3 %all_to_all.24 = bf16[3,72,32,576]{3,1,0,2:T(8,128)(2,1)S(1)} all-to-all(bf16[3,72,32,576]{3,1,0,2:T(8,128)(2,1)} %copy.133), channel_id=1, replica_groups=mesh['rows'=2,'seq'=16] {'rows','seq'}, dimensions={2} | all-to-all | bytes 15925248 | tf_op jit(solution)/shard_map/all_to_all | solution.py:96
  681.5 12.7 multiply_convert_fusion.1
  695.6 10.8 convolution_bitcast_fusion
  707.2 191.9 %reduce-scatter.6.cloned.1.call-done = f32[1,128,2304]{2,1,0:T(8,128)} async-done(((f32[1,2048,2304]{2,1,0:T(8,128)}), f32[1,128,2304]{2,1,0:T(8,128)}) %reduce-scatter.6.cloned.1.call-update) | async-done | bytes 1179664 | tf_op jit(solution)/shard_map/reduce_scatter | solution.py:160
  906.5 78.9 %all-gather.21.cloned.1.call-done = bf16[1,2048,2304]{2,1,0:T(8,128)(2,1)} async-done(((bf16[1,128,2304]{2,1,0:T(8,128)(2,1)}), bf16[1,2048,2304]{2,1,0:T(8,128)(2,1)}) %all-gather.21.cloned.1.call-update) | async-done | bytes 9437200 | tf_op jit(solution)/shard_map/all_gather | solution.py:168
  985.3 16.0 multiply_convert_fusion
  1001.3 10.8 fusion.172
  1012.1 19.5 add_bitcast_fusion
  1043.6 190.7 %reduce-scatter.8.cloned.1.call-done = f32[1,128,2304]{2,1,0:T(8,128)} async-done(((f32[1,2048,2304]{2,1,0:T(8,128)}), f32[1,128,2304]{2,1,0:T(8,128)}) %reduce-scatter.8.cloned.1.call-update) | async-done | bytes 1179664 | tf_op jit(solution)/shard_map/reduce_scatter | solution.py:178
  1244.5 41.7 %all-gather.25.cloned.1.call-done = bf16[1,2048,4,256]{3,1,2,0:T(8,128)(2,1)} async-done(((bf16[1,128,4,256]{3,1,2,0:T(8,128)(2,1)}), bf16[1,2048,4,256]{3,1,2,0:T(8,128)(2,1)}) %all-gather.25.cloned.1.call-update) | async-done | bytes 4194320 | tf_op jit(solution)/shard_map/all_gather | solution.py:216
  1300.4 9.9 convolution_bitcast_fusion.1
  1342.9 60.7 %reduce-scatter.10.cloned.1.call-done = f32[1,128,4,256]{3,1,2,0:T(8,128)} async-done(((f32[1,2048,4,256]{3,1,2,0:T(8,128)}), f32[1,128,4,256]{3,1,2,0:T(8,128)}) %reduce-scatter.10.cloned.1.call-update) | async-done | bytes 524304 | tf_op jit(solution)/shard_map/reduce_scatter | solution.py:244
  1404.9 107.4 %reduce-scatter.12.cloned.1.call-done = f32[1,128,4,256]{1,3,2,0:T(8,128)} async-done(((f32[1,2048,4,256]{1,3,2,0:T(8,128)}), f32[1,128,4,256]{1,3,2,0:T(8,128)}) %reduce-scatter.12.cloned.1.call-update) | async-done | bytes 524304 | tf_op jit(solution)/shard_map/reduce_scatter | solution.py:245
  1529.4 132.7 %concatenate.74 = f32[2304,6272]{0,1:T(8,128)} concatenate(f32[2304,2048]{0,1:T(8,128)} %fusion.123, f32[2304,1024]{0,1:T(8,128)} %fusion.125, f32[2304,1024]{0,1:T(8,128)} %fusion.121, f32[2304,2048]{0,1:T(8,128)} %fusion.175, f32[2304,1]{0,1:T(1,128)S(1)} %stack.40, f32[2304,1]{0,1:T(1,128)S(1)} %copy-done.33, f32[2304,1]{0,1:T(1,128)S(1)} %copy-done.32, ...), dimensions={1} | concatenate | bytes 115605504 | tf_op jit(solution)/shard_map/concatenate | solution.py:269
  1663.8 9.8 fusion.20
  1673.6 10.1 fusion.24
  1693.5 19.6 copy.147
  1717.5 380.9 %all-to-all-done.1 = bf16[3,2304,1,576]{3,0,2,1:T(4,128)(2,1)} async-done(((bf16[3,2304,1,576]{3,0,2,1:T(4,128)(2,1)}), bf16[3,2304,1,576]{3,0,2,1:T(4,128)(2,1)}, u32[]{:S(2)}, u32[]{:S(2)}) %all-to-all-start.1) | async-done | bytes 7962656 | tf_op jit(solution)/shard_map/all_to_all | solution.py:188
  2098.3 9.6 copy.148
  2107.9 11.0 convert.36
  2118.9 12.2 reduce_sum.170
  2158.7 573.3 %all-reduce.3.cloned.1.call-done = f32[2304,6272]{0,1:T(8,128)} async-done(((f32[2304,6272]{0,1:T(8,128)}), f32[2304,6272]{0,1:T(8,128)}) %all-reduce.3.cloned.1.call-update) | async-done | bytes 57802768
  (245 shorter events, 247.0 us)
Async XLA Ops:
  7.2 73.9 %copy-start = (bf16[1,128,2304]{2,1,0:T(8,128)(2,1)S(1)}, bf16[1,128,2304]{2,1,0:T(8,128)(2,1)}, u32[]{:S(2)}) copy-start(bf16[1,128,2304]{2,1,0:T(8,128)(2,1)} %param.15) | copy-start | bytes 1769476
  7.2 24.2 copy-start.36
  7.2 73.9 %all-gather.13.cloned.1.call-start = ((), (), s32[]{:S(2)}) async-start(), calls=%async_computation.7 | async-start | bytes 4866048 | tf_op jit(solution)/shard_map/all_gather | solution.py:86
  14.7 132.3 %all-gather.11.cloned.1.call-start = ((), (), s32[]{:S(2)}) async-start(), calls=%async_computation.6 | async-start | bytes 4866048 | tf_op jit(solution)/shard_map/all_gather | solution.py:85
  20.6 210.9 %all-gather.17.cloned.1.call-start = ((), (), s32[]{:S(2)}) async-start(), calls=%async_computation.9 | async-start | bytes 9732096 | tf_op jit(solution)/shard_map/all_gather | solution.py:84
  30.1 277.6 %all-gather.15.cloned.1.call-start = ((), (), s32[]{:S(2)}) async-start(), calls=%async_computation.8 | async-start | bytes 8912896 | tf_op jit(solution)/shard_map/all_gather | solution.py:137
  31.4 212.8 %copy-start.34 = (f32[128]{0:T(128)}, f32[128]{0:T(128)S(1)}, u32[]{:S(2)}) copy-start(f32[128]{0:T(128)S(1)} %fusion.144) | copy-start | bytes 1540
  31.5 212.8 %copy-start.24 = (f32[2304]{0:T(1024)}, f32[2304]{0:T(1024)S(1)}, u32[]{:S(2)}) copy-start(f32[2304]{0:T(1024)S(1)} %broadcast_add_fusion.3) | copy-start | bytes 27652
  84.6 73.3 %copy-start.15 = (bf16[1,128,4,256]{3,1,2,0:T(8,128)(2,1)}, bf16[1,128,4,256]{3,1,2,0:T(8,128)(2,1)S(1)}, u32[]{:S(2)}) copy-start(bf16[1,128,4,256]{3,1,2,0:T(8,128)(2,1)S(1)} %copy.129) | copy-start | bytes 786436
  157.7 14.9 copy-start.40
  157.8 14.9 copy-start.37
  157.8 14.9 copy-start.38
  157.8 15.9 copy-start.13
  159.5 231.8 %all-gather.19.cloned.1.call-start = ((), (), s32[]{:S(2)}) async-start(), calls=%async_computation.10 | async-start | bytes 9732096 | tf_op jit(solution)/shard_map/all_gather | solution.py:87
  168.6 503.4 %all-gather.27.cloned.1.call-start = ((), (), s32[]{:S(2)}) async-start(), calls=%async_computation.18 | async-start | bytes 10027008 | tf_op jit(solution)/shard_map/all_gather | solution.py:155
  172.6 28.4 %copy-start.14 = (s32[72,9216]{1,0:T(8,128)S(1)}, s32[72,9216]{1,0:T(8,128)}, u32[]{:S(2)}) copy-start(s32[72,9216]{1,0:T(8,128)} %param.25) | copy-start | bytes 7962628
  244.3 63.4 %copy-start.29 = (pred[128,2048]{0,1:T(8,128)(4,1)S(1)}, pred[128,2048]{0,1:T(8,128)(4,1)}, u32[]{:S(2)}) copy-start(pred[128,2048]{0,1:T(8,128)(4,1)} %fusion.103) | copy-start | bytes 786436
  316.3 81.9 %copy-start.16 = (bf16[1,128,4,2,256]{1,4,3,2,0:T(8,128)(2,1)}, bf16[1,128,4,2,256]{1,4,3,2,0:T(8,128)(2,1)S(1)}, u32[]{:S(2)}) copy-start(bf16[1,128,4,2,256]{1,4,3,2,0:T(8,128)(2,1)S(1)} %get-tuple-element.126) | copy-start | bytes 1572868
  399.7 499.4 %reduce-scatter.6.cloned.1.call-start = ((), (), s32[]{:S(2)}) async-start(), calls=%async_computation.11 | async-start | bytes 20054016 | tf_op jit(solution)/shard_map/reduce_scatter | solution.py:160
  706.5 194.2 %copy-start.6 = (bf16[1,128,2304]{2,1,0:T(8,128)(2,1)S(1)}, bf16[1,128,2304]{2,1,0:T(8,128)(2,1)}, u32[]{:S(2)}) copy-start(bf16[1,128,2304]{2,1,0:T(8,128)(2,1)} %param.16) | copy-start | bytes 1769476
  706.5 278.8 %all-gather.21.cloned.1.call-start = ((), (), s32[]{:S(2)}) async-start(), calls=%async_computation.12 | async-start | bytes 10027008 | tf_op jit(solution)/shard_map/all_gather | solution.py:168
  904.6 132.2 %all-gather.23.cloned.1.call-start = ((), (), s32[]{:S(2)}) async-start(), calls=%async_computation.14 | async-start | bytes 4456448 | tf_op jit(solution)/shard_map/all_gather | solution.py:215
  906.4 327.8 %reduce-scatter.8.cloned.1.call-start = ((), (), s32[]{:S(2)}) async-start(), calls=%async_computation.13 | async-start | bytes 20054016 | tf_op jit(solution)/shard_map/reduce_scatter | solution.py:178
  985.3 16.0 copy-start.11
  1031.6 254.6 %all-gather.25.cloned.1.call-start = ((), (), s32[]{:S(2)}) async-start(), calls=%async_computation.15 | async-start | bytes 4456448 | tf_op jit(solution)/shard_map/all_gather | solution.py:216
  1032.3 371.3 %reduce-scatter.10.cloned.1.call-start = ((), (), s32[]{:S(2)}) async-start(), calls=%async_computation.16 | async-start | bytes 8912896 | tf_op jit(solution)/shard_map/reduce_scatter | solution.py:244
  1238.0 48.2 %copy-start.30 = (pred[128,2048]{0,1:T(8,128)(4,1)S(1)}, pred[128,2048]{0,1:T(8,128)(4,1)}, u32[]{:S(2)}) copy-start(pred[128,2048]{0,1:T(8,128)(4,1)} %fusion.103) | copy-start | bytes 786436
  1300.4 211.9 %reduce-scatter.12.cloned.1.call-start = ((), (), s32[]{:S(2)}) async-start(), calls=%async_computation.17 | async-start | bytes 8912896 | tf_op jit(solution)/shard_map/reduce_scatter | solution.py:245
  1310.3 1421.6 %all-reduce.3.cloned.1.call-start = ((), (), s32[]{:S(2)}) async-start(), calls=%async_computation.19 | async-start | bytes 115605504
  1663.8 20.0 slice-start.4
  1663.8 20.0 slice-start.5
  1713.1 385.2 %all-to-all-start.1 = ((bf16[3,2304,1,576]{3,0,2,1:T(4,128)(2,1)}), bf16[3,2304,1,576]{3,0,2,1:T(4,128)(2,1)}, u32[]{:S(2)}, u32[]{:S(2)}) async-start(bf16[3,2304,1,576]{3,0,2,1:T(4,128)(2,1)} %copy.147), calls=%async_computation.5 | async-start | bytes 23592960 | tf_op jit(solution)/shard_map/all_to_all | solution.py:188
  (41 other events, 244.1 us)
Sparse Core Ops, SparseCore 0:
  14.8 66.2 all-gather.12
  84.5 62.3 all-gather.10
  150.4 81.0 all-gather.16
  234.1 73.4 all-gather.14
  311.0 80.2 all-gather.18
  399.8 95.4 all-gather.26
  706.6 192.4 reduce-scatter.5
  904.8 80.5 all-gather.20
  988.1 48.7 all-gather.22
  1040.8 193.4 reduce-scatter.7
  1236.5 49.6 all-gather.24
  1300.5 103.0 reduce-scatter.9
  1407.7 104.5 reduce-scatter.11
  1662.2 1069.6 all-reduce.2
